TPU v7x, 512 devices: a whole 4x8x8 slice. The times are simulated.
512 devices in a mesh: cells: 128 (over y, z, core), samp: 4 (over x).
Axes of the slice: x: 4, y: 8, z: 8, core: 2. Of those that a mesh axis runs over, the one named last changes fastest.
Arguments:
- snapshots: bfloat16 [262144, 4096], P('cells', 'samp'), may hold values from -24 to 24
- left_slow: bfloat16 [120, 4096], P(None, 'cells'), may hold values from -0.09375 to 0.09375
- left_fast: bfloat16 [120, 64], replicated, may hold values from -0.75 to 0.75
- right_slow: bfloat16 [150, 128], P(None, 'samp'), may hold values from -0.5 to 0.5
- right_fast: bfloat16 [150, 32], replicated, may hold values from -1 to 1
Outputs:
- range_sketch: float32 [262144, 150], P(('cells', 'samp'))
- core: float32 [150, 4096], P(None, ('samp', 'cells'))
All inputs are finite; a program needn't handle non-finite values.
Results may differ from a plain program's by a relative error of at most 0.012.
The roundings to bfloat16 on the way count: a program that leaves them out, or rounds other values in their place, can miss the bound.
Values sent between devices are 32-bit elements; how exact they have to be, the bound alone decides.
A program may use at most 64 MiB of HBM per device.

v0:
```python
import jax
import jax.numpy as jnp
from jax import lax
from jax.sharding import PartitionSpec as P


def expand(slow, fast):
    rows = slow.shape[0]
    return (
        (slow.astype(jnp.float32)[:, :, None] * fast.astype(jnp.float32)[:, None, :])
        .reshape(rows, -1)
        .astype(jnp.bfloat16)
    )


def on_device(snapshots, left_slow, left_fast, right_slow, right_fast):
    psi = expand(left_slow, left_fast)
    omega = expand(right_slow, right_fast)
    left_term = jnp.dot(psi, snapshots, preferred_element_type=jnp.float32)
    range_term = lax.dot_general(
        snapshots, omega, (((1,), (1,)), ((), ())), preferred_element_type=jnp.float32
    )
    range_part = lax.psum_scatter(range_term, "samp", scatter_dimension=0, tiled=True)
    width = snapshots.shape[1] // lax.axis_size("cells")
    col_start = lax.axis_index("cells") * width
    left_full = lax.psum(left_term, "cells")
    left_part = lax.dynamic_slice_in_dim(left_full, col_start, width, 1)
    height = range_part.shape[0]
    psi_rows = lax.dynamic_slice_in_dim(psi, lax.axis_index("samp") * height, height, 1).astype(
        jnp.float32
    )
    partial_value = jnp.dot(psi_rows, range_part, precision=lax.Precision.HIGHEST)
    core_input = lax.psum(partial_value, ("cells", "samp"))
    rank_left = core_input.shape[0]
    gram = jnp.dot(core_input, core_input.T, precision=lax.Precision.HIGHEST) + 0.5 * jnp.eye(
        rank_left, dtype=jnp.float32
    )
    factor = jnp.linalg.cholesky(gram)
    solved = jax.scipy.linalg.cho_solve((factor, True), left_part)
    core = jnp.dot(core_input.T, solved, precision=lax.Precision.HIGHEST)
    return (range_part, core)


def solution(mesh):
    placed = (P("cells", "samp"), P(None, "cells"), P(), P(None, "samp"), P())
    return jax.shard_map(
        on_device,
        mesh=mesh,
        in_specs=placed,
        out_specs=(P(("cells", "samp"), None), P(None, ("samp", "cells"))),
        check_vma=False,
    )
```

profile of v0, /device:TPU:1, one launch (start us, length us, event | category | flops | bytes accessed | tf_op | source)
XLA Modules:
  0.0 516.8 jit_solution(6661757169224194869)
XLA Ops:
  7.2 0.0 copy-start
  7.2 0.0 copy-start.1
  7.2 0.0 reduce-scatter.2.cloned.1.call-start
  7.2 0.7 convert_element_type.27
  8.0 0.7 convert_element_type.26
  8.7 0.1 multiply_convert_fusion.1
  8.8 4.8 convolution_bitcast_fusion
  13.6 0.0 reduce-scatter.2.cloned.1.call-update
  13.6 0.0 all-reduce.3.cloned.1.call-start
  13.7 0.0 copy-done
  13.7 0.0 copy-done.1
  13.7 0.1 multiply_convert_fusion
  13.9 33.1 %reduce-scatter.2.cloned.1.call-done = f32[512,150]{0,1:T(8,128)} async-done(((f32[2048,150]{0,1:T(8,128)}), f32[512,150]{0,1:T(8,128)}) %reduce-scatter.2.cloned.1.call-update) | async-done | bytes 307216 | tf_op jit(solution)/shard_map/reduce_scatter | solution.py:23
  46.9 1.9 fusion
  48.8 0.0 all-reduce.3.cloned.1.call-update
  48.9 0.0 all-reduce.5.cloned.1.call-start
  48.9 3.7 fusion.13
  52.6 0.0 all-reduce.5.cloned.1.call-update
  52.6 264.9 %all-reduce.3.cloned.1.call-done = f32[120,150]{0,1:T(8,128)} async-done(((f32[120,150]{0,1:T(8,128)}), f32[120,150]{0,1:T(8,128)}) %all-reduce.3.cloned.1.call-update) | async-done | bytes 72016 | tf_op jit(solution)/shard_map/psum | solution.py:33
  317.5 1.4 fusion.12
  318.9 0.1 copy.12
  319.0 11.0 %cholesky.16 = f32[120,120]{1,0:T(8,128)S(1)} custom-call(f32[120,120]{1,0:T(8,128)S(1)} %fusion.8), custom_call_target="Cholesky" | custom-call | tf_op jit(solution)/shard_map/jit(cholesky)/cholesky | solution.py:38
  330.1 0.6 compare_reduce_fusion
  330.7 0.7 fusion.2
  331.4 9.2 %custom-call.10 = f32[1,120,120]{1,2,0:T(8,128)S(1)} custom-call(f32[1,120,120]{2,1,0:T(8,128)S(1)} %fusion.2), custom_call_target="InvertDiagBlocksLowerTriangular" | custom-call | tf_op jit(solution)/shard_map/jit(_cho_solve)/triangular_solve | solution.py:39
  340.6 166.5 %all-reduce.5.cloned.1.call-done = f32[120,1024]{1,0:T(8,128)} async-done(((f32[120,1024]{1,0:T(8,128)}), f32[120,1024]{1,0:T(8,128)}) %all-reduce.5.cloned.1.call-update) | async-done | bytes 491536 | tf_op jit(solution)/shard_map/psum | solution.py:26
  507.1 1.2 fusion.5
  508.3 0.3 fusion.3
  508.6 1.8 fusion.14
  (4 shorter events, 0.1 us)
Async XLA Ops:
  7.2 6.5 %copy-start = (bf16[120,64]{0,1:T(8,128)(2,1)S(1)}, bf16[120,64]{0,1:T(8,128)(2,1)}, u32[]{:S(2)}) copy-start(bf16[120,64]{0,1:T(8,128)(2,1)} %param.7) | copy-start | bytes 46084
  7.2 6.5 %copy-start.1 = (bf16[120,32]{0,1:T(8,128)(2,1)S(1)}, bf16[120,32]{0,1:T(8,128)(2,1)}, u32[]{:S(2)}) copy-start(bf16[120,32]{0,1:T(8,128)(2,1)} %param.6) | copy-start | bytes 23044
  7.2 39.8 %reduce-scatter.2.cloned.1.call-start = ((), (), s32[]{:S(2)}) async-start(), calls=%async_computation.1 | async-start | bytes 1556480 | tf_op jit(solution)/shard_map/reduce_scatter | solution.py:23
  13.6 303.9 %all-reduce.3.cloned.1.call-start = ((), (), s32[]{:S(2)}) async-start(), calls=%async_computation.2 | async-start | bytes 155648 | tf_op jit(solution)/shard_map/psum | solution.py:33
  48.9 458.3 %all-reduce.5.cloned.1.call-start = ((), (), s32[]{:S(2)}) async-start(), calls=%async_computation.3 | async-start | bytes 983040 | tf_op jit(solution)/shard_map/psum | solution.py:26
Sparse Core Ops, SparseCore 0:
  13.7 33.1 reduce-scatter.1
  51.9 265.5 all-reduce.2
  320.8 186.2 all-reduce.4
where the time goes:
time: 518 us; the launch traced here: 517 us
  waiting for transfers between devices  465 us (90%)
  other arithmetic  23.2 us (4%)
  matrix products  15 us (3%)
  between operations  13.9 us (3%)
    psum x1, waiting for transfers between devices, on_device(): core_input = lax.psum(partial_value, ('cells', 'samp'))  265 us
    psum x1, waiting for transfers between devices, on_device(): left_full = lax.psum(left_term, 'cells')  167 us
    reduce_scatter x1, waiting for transfers between devices, on_device(): lax.psum_scatter(range_term, 'samp', scatter_dimension=0, tiled=True)  33.1 us
    another operation x3, other arithmetic, on_device(): factor = jnp.linalg.cholesky(gram)  11.6 us
  transfers between devices with their start and end apart: 3, of which 3 were waited for; matrix products, arithmetic and copies ran while one was open for 5% of the time, Pallas kernels for 0%

commit v1 on v0

v1 whole, which is shorter than its diff:
```python
import functools

import jax
import jax.numpy as jnp
from jax import lax
from jax.experimental import pallas as pl
from jax.experimental.pallas import tpu as pltpu
from jax.sharding import PartitionSpec as P

F32 = jnp.float32
BF16 = jnp.bfloat16
MESH = pl.DeviceIdType.MESH
NY, NZ = 8, 8
LP, RP = 128, 256
HIGHEST = lax.Precision.HIGHEST


def dot(a, b, dims, precision=None):
    return lax.dot_general(a, b, (dims, ((), ())), precision=precision, preferred_element_type=F32)


def expand_rows(slow_t, fast_t, width, start):
    ns, nf = slow_t.shape[0], fast_t.shape[0]
    n = lax.broadcasted_iota(jnp.int32, (ns, width), 1) + start
    a = lax.broadcasted_iota(jnp.int32, (ns, width), 0)
    pick_slow = jnp.where(n // nf == a, 1.0, 0.0).astype(BF16)
    n = lax.broadcasted_iota(jnp.int32, (nf, width), 1) + start
    b = lax.broadcasted_iota(jnp.int32, (nf, width), 0)
    pick_fast = jnp.where(n % nf == b, 1.0, 0.0).astype(BF16)
    dims = ((0,), (0,))
    return (dot(slow_t, pick_slow, dims) * dot(fast_t, pick_fast, dims)).astype(BF16)


def compute_kernel(x_ref, ls_ref, lf_ref, rs_ref, rf_ref, rt_ref, lt_ref, cp_ref, omega, acc):
    step = pl.program_id(0)
    rows, samples = x_ref.shape
    rank_l = ls_ref.shape[1]
    rank_r = rs_ref.shape[1]

    @pl.when(step == 0)
    def _():
        omega[...] = expand_rows(rs_ref[...], rf_ref[...], samples, 0)
        acc[...] = jnp.zeros_like(acc)
        cp_ref[...] = jnp.zeros_like(cp_ref)

    x = x_ref[...]
    psi = expand_rows(ls_ref[...], lf_ref[...], rows, step * rows)
    acc[0:rank_l, :] += dot(psi, x, ((1,), (0,)))
    rt_ref[0] = dot(omega[...], x, ((1,), (1,)))

    @pl.when(step == pl.num_programs(0) - 1)
    def _():
        left = acc[...]
        hi = left.astype(BF16)
        rest = left - hi.astype(F32)
        mid = rest.astype(BF16)
        low = (rest - mid.astype(F32)).astype(BF16)
        dims = ((1,), (1,))
        om = omega[...]
        cp_ref[:, 0:rank_r] = dot(hi, om, dims) + (dot(mid, om, dims) + dot(low, om, dims))
        left_t = left.T
        for j in range(samples // 8):
            lt_ref[j % 2, j // (2 * NZ), (j // 2) % NZ] = left_t[8 * j : 8 * j + 8, :]


def exchange_kernel(
    nx,
    rt, lt, cp,
    c_out, l_out, r_out,
    cc, lc, cs, ls, cy, ly, cq, cz, cr, cx, cf, lz, lq, ra, rb, rl, rr,
    ssem, rsem,
):
    cell = lax.axis_index("cells")
    x = lax.axis_index("samp")
    c = lax.rem(cell, 2)
    z = lax.rem(cell // 2, NZ)
    y = cell // (2 * NZ)

    def at(y_, z_, c_, x_):
        return ((y_ * NZ + z_) * 2 + c_, x_)

    other = at(y, z, 1 - c, x)
    ys = [lax.rem(y + d, NY) for d in range(1, NY)]
    zs = [lax.rem(z + d, NZ) for d in range(1, NZ)]
    xs = [lax.rem(x + d, nx) for d in range(1, nx)]
    to_y = [at(p, z, c, x) for p in ys]
    to_z = [at(y, p, c, x) for p in zs]
    to_x = [at(y, z, c, p) for p in xs]

    barrier = pltpu.get_barrier_semaphore()
    peers = [other] + to_y + to_z + to_x
    for peer in peers:
        pl.semaphore_signal(barrier, inc=1, device_id=peer, device_id_type=MESH)
    pl.semaphore_wait(barrier, len(peers))

    used = [0]
    sent = []

    def send(src, dst, peer):
        k = used[0]
        used[0] += 1
        copy = pltpu.make_async_remote_copy(
            src_ref=src, dst_ref=dst, send_sem=ssem.at[k], recv_sem=rsem.at[k],
            device_id=peer, device_id_type=MESH,
        )
        copy.start()
        sent.append(copy)
        return copy

    def arrived(copies):
        for copy in copies:
            copy.wait_recv()

    half = rt.shape[2] // 2
    lo, hi = pl.ds(0, half), pl.ds(half, half)
    right, left = to_x[0], to_x[-1]

    g_cc = [send(cp.at[1 - c], cc, other)]
    g_lc = [send(lt.at[1 - c], lc, other)]
    far = lax.rem(x + 2, nx)
    g_ra = [send(rt.at[far, :, lo], ra, right)]
    g_rb = [send(rt.at[far, :, hi], rb, left)]

    arrived(g_cc)
    cs[...] = cp[c] + cc[...]
    g_cy = [send(cs.at[ys[i]], cy.at[i], to_y[i]) for i in range(NY - 1)]

    arrived(g_lc)
    ls[...] = lt[c] + lc[...]
    g_ly = [send(ls.at[ys[i]], ly.at[i], to_y[i]) for i in range(NY - 1)]

    arrived(g_ra)
    xr, xl = xs[0], xs[-1]
    rl[:, lo] = rt[xr, :, lo] + ra[...]
    rl[:, hi] = rt[xr, :, hi]
    arrived(g_rb)
    rr[:, lo] = rt[xl, :, lo]
    rr[:, hi] = rt[xl, :, hi] + rb[...]
    from_left, from_right = cx_refs = (r_out.at[0], r_out.at[1])
    g_r = [send(rl, from_left, right), send(rr, from_right, left)]

    arrived(g_cy)
    cq[...] = cs[y] + functools.reduce(lambda a, b: a + b, [cy[i] for i in range(NY - 1)])
    g_cz = [send(cq, cz.at[i], to_z[i]) for i in range(NZ - 1)]
    arrived(g_cz)
    cr[...] = cq[...] + functools.reduce(lambda a, b: a + b, [cz[i] for i in range(NZ - 1)])
    g_cx = [send(cr, cx.at[i], to_x[i]) for i in range(nx - 1)]
    arrived(g_cx)
    cf[c, y] = cr[...] + functools.reduce(lambda a, b: a + b, [cx[i] for i in range(nx - 1)])
    g_ag = [send(cf.at[c, y], cf.at[c, y], to_y[i]) for i in range(NY - 1)]

    arrived(g_ly)
    lq[...] = ls[y] + functools.reduce(lambda a, b: a + b, [ly[i] for i in range(NY - 1)])
    g_lz = [send(lq.at[zs[i]], lz.at[i], to_z[i]) for i in range(NZ - 1)]

    arrived(g_ag)
    g_ac = [send(cf.at[c], cf.at[c], other)]

    arrived(g_lz)
    l_out[...] = lq[z] + functools.reduce(lambda a, b: a + b, [lz[i] for i in range(NZ - 1)])
    arrived(g_r)
    r_out[2] = rt[x]
    arrived(g_ac)
    c_out[...] = cf[...]
    for copy in sent:
        copy.wait_send()


def rows_of(a, t):
    return jnp.broadcast_to(a[t : t + 1, :], (8, LP))


def lanes_of(a, t):
    return jnp.broadcast_to(a[:, t : t + 1], (8, LP))


def solve_kernel(rank_l, c_ref, l_ref, r_ref, core_ref, range_ref):
    cm = c_ref[...]
    gram = dot(cm, cm, ((1,), (1,)), HIGHEST)
    row = lax.broadcasted_iota(jnp.int32, (LP, LP), 0)
    col = lax.broadcasted_iota(jnp.int32, (LP, LP), 1)
    gram = gram + jnp.where(row == col, 0.5, 0.0)
    sub = lax.broadcasted_iota(jnp.int32, (8, LP), 0)
    lane = lax.broadcasted_iota(jnp.int32, (8, LP), 1)

    tiles = [gram[8 * i : 8 * i + 8, :] for i in range(LP // 8)]
    rhs = l_ref[...]
    panels = rank_l // 8
    for kb in range(panels):
        base = 8 * kb
        p = tiles[kb]
        cols = [lanes_of(p, base + t) for t in range(8)]
        for t in range(8):
            ct = cols[t]
            inv = 1.0 / rows_of(ct, t)
            here = lane == base + t
            prow = jnp.where(here, inv, rows_of(p, t) * inv)
            p = jnp.where(sub == t, prow, jnp.where(here, 0.0, p) - ct * prow)
            for j in range(t + 1, 8):
                crow = rows_of(cols[j], t) * inv
                cols[j] = jnp.where(sub == t, crow, cols[j] - ct * crow)
        inside = (lane >= base) & (lane < base + 8)
        w = jnp.where(inside, -p, p)
        ws = [rows_of(w, t) for t in range(8)]

        def update(a):
            terms = [lanes_of(a, base + t) * ws[t] for t in range(8)]
            while len(terms) > 1:
                terms = [terms[i] + terms[i + 1] for i in range(0, len(terms), 2)]
            return jnp.where(inside, 0.0, a) - terms[0]

        for i in range(kb + 1, panels):
            tiles[i] = update(tiles[i])
        rhs = update(rhs)
    core = dot(rhs, cm, ((1,), (0,)), HIGHEST)
    core_ref[...] = core[:, 0 : core_ref.shape[1]]
    range_ref[...] = r_ref[2] + (r_ref[0] + r_ref[1])


VMEM = pl.BlockSpec(memory_space=pltpu.VMEM)


def on_device(snapshots, left_slow, left_fast, right_slow, right_fast):
    nx = lax.axis_size("samp")
    rows, samples = snapshots.shape
    rank_l, rank_r = left_slow.shape[0], right_slow.shape[0]
    part = rows // nx
    pr = LP // (2 * NY)
    whole = lambda a: pl.BlockSpec(a.shape, lambda i: (0,) * len(a.shape))
    f32 = lambda *shape: jax.ShapeDtypeStruct(shape, F32)
    small = [left_slow.T, left_fast.T, right_slow.T, right_fast.T]
    lt_shape, cp_shape = f32(2, NY, NZ, 8, LP), f32(LP, RP)
    rt, lt, cp = pl.pallas_call(
        compute_kernel,
        grid=(nx,),
        in_specs=[pl.BlockSpec((part, samples), lambda i: (i, 0))] + [whole(a) for a in small],
        out_specs=(
            pl.BlockSpec((1, rank_r, part), lambda i: (i, 0, 0)),
            whole(lt_shape),
            whole(cp_shape),
        ),
        out_shape=(f32(nx, rank_r, part), lt_shape, cp_shape),
        scratch_shapes=[pltpu.VMEM((rank_r, samples), BF16), pltpu.VMEM((LP, samples), F32)],
        name="sketch",
    )(snapshots, *small)

    copies = 2 + 4 + 3 * (NY - 1) + 2 * (NZ - 1) + (nx - 1) + 1
    vm = lambda *shape: pltpu.VMEM(shape, F32)
    cf, lf, rf = pl.pallas_call(
        functools.partial(exchange_kernel, nx),
        in_specs=[VMEM] * 3,
        out_specs=(VMEM,) * 3,
        out_shape=(f32(2, NY, pr, RP), f32(8, LP), f32(3, rank_r, part)),
        scratch_shapes=[
            vm(NY, pr, RP), vm(NY, NZ, 8, LP), vm(NY, pr, RP), vm(NY, NZ, 8, LP),
            vm(NY - 1, pr, RP), vm(NY - 1, NZ, 8, LP),
            vm(pr, RP), vm(NZ - 1, pr, RP), vm(pr, RP), vm(nx - 1, pr, RP), vm(2, NY, pr, RP),
            vm(NZ - 1, 8, LP), vm(NZ, 8, LP),
            vm(rank_r, part // 2), vm(rank_r, part // 2), vm(rank_r, part), vm(rank_r, part),
            pltpu.SemaphoreType.DMA((copies,)), pltpu.SemaphoreType.DMA((copies,)),
        ],
        compiler_params=pltpu.CompilerParams(collective_id=0, has_side_effects=True),
        name="exchange",
    )(rt, lt, cp.reshape(2, NY, pr, RP))

    core_t, range_t = pl.pallas_call(
        functools.partial(solve_kernel, rank_l),
        in_specs=[VMEM] * 3,
        out_specs=(VMEM,) * 2,
        out_shape=(f32(8, rank_r), f32(rank_r, part)),
        name="solve",
    )(cf.reshape(LP, RP), lf, rf)
    return (range_t.T, core_t.T)


def solution(mesh):
    placed = (P("cells", "samp"), P(None, "cells"), P(), P(None, "samp"), P())
    return jax.shard_map(
        on_device,
        mesh=mesh,
        in_specs=placed,
        out_specs=(P(("cells", "samp"), None), P(None, ("samp", "cells"))),
        check_vma=False,
    )
```

time: 518 us -> 54.3 us (0.10)
  waiting for transfers between devices: 465 us -> 0 us
  Pallas kernels: 0 us -> 53.4 us
  other arithmetic: 23.2 us -> 0 us
  matrix products: 15 us -> 0 us
  between operations: 13.9 us -> 0.64 us
    psum x2 -> x0, waiting for transfers between devices: 431 us -> none  [the longest x1 265 us: on_device(): core_input = lax.psum(partial_value, ('cells', 'samp'))]
    pallas_call x0 -> x3, Pallas kernels: none -> 53.4 us  [the longest x1 39.5 us: on_device(): pl.pallas_call(functools.partial(exchange_kernel, nx), in_specs=[VMEM] *...]
    reduce_scatter x1 -> x0, waiting for transfers between devices: 33.1 us -> none  [on_device(): lax.psum_scatter(range_term, 'samp', scatter_dimension=0, tiled=True)]
    another operation x5 -> x0, other arithmetic: 21.5 us -> none  [the longest x3 11.6 us: on_device(): factor = jnp.linalg.cholesky(gram)]
    dot_general x5 -> x0, matrix products: 13.5 us -> none  [the longest x1 4.8 us: on_device(): lax.dot_general(snapshots, omega, (((1,), (1,)), ((), ())), preferred_ele...]
  transfers between devices with their start and end apart: 3 -> 0, of which waited for: 3 -> 0; matrix products, arithmetic and copies ran while one was open for 5% -> 0% of each run, Pallas kernels for 0% -> 0%
where the time goes in v1:
time: 54.3 us; the launch traced here: 54 us
  Pallas kernels  53.4 us (98%)
  between operations  0.64 us (1%)
    pallas_call x1, Pallas kernels, on_device(): pl.pallas_call(functools.partial(exchange_kernel, nx), in_specs=[VMEM] *...  39.5 us
    pallas_call x1, Pallas kernels, on_device(): pl.pallas_call(compute_kernel, grid=(nx,), in_specs=[pl.BlockSpec((part,...  7.03 us
    pallas_call x1, Pallas kernels, on_device(): pl.pallas_call(functools.partial(solve_kernel, rank_l), in_specs=[VMEM] *...  6.81 us

profile of v1, /device:TPU:1, one launch (start us, length us, event | category | flops | bytes accessed | tf_op | source)
XLA Modules:
  0.0 54.0 jit_solution(11314352081099016799)
XLA Ops:
  0.6 7.0 %sketch.1 = (f32[4,150,512]{2,1,0:T(8,128)}, f32[2,8,8,8,128]{4,3,2,1,0:T(8,128)}, f32[128,256]{1,0:T(8,128)}) custom-call(bf16[2048,1024]{1,0:T(8,128)(2,1)} %x_ref.1, bf16[32,120]{1,0:T(8,128)(2,1)} %bitcast.13, bf16[64,120]{1,0:T(8,128)(2,1)} %bitcast.10, bf16[32,150]{1,0:T(8,128)(2,1)} %bitcast.11, bf16[32,150]{1,0:T(8,128)(2,1)} %bitcast.12), custom_call_target="tpu_custom_call" | custom-call | tf_op jit(solution)/shard_map/sketch/pallas_call | solution.py:233
  7.7 39.5 %exchange.1 = (f32[2,8,8,256]{3,2,1,0:T(8,128)}, f32[8,128]{1,0:T(8,128)}, f32[3,150,512]{2,1,0:T(8,128)}) custom-call(f32[4,150,512]{2,1,0:T(8,128)} %get-tuple-element.10.rt, f32[2,8,8,8,128]{4,3,2,1,0:T(8,128)} %get-tuple-element.11.lt, f32[2,8,8,256]{3,2,1,0:T(8,128)} %bitcast.9), custom_call_target="tpu_custom_call" | custom-call | tf_op jit(solution)/shard_map/exchange/pallas_call | solution.py:249
  47.2 6.8 %solve.1 = (f32[8,150]{1,0:T(8,128)}, f32[150,512]{1,0:T(8,128)}) custom-call(f32[128,256]{1,0:T(8,128)} %bitcast.8, f32[8,128]{1,0:T(8,128)} %get-tuple-element.14.l_ref, f32[3,150,512]{2,1,0:T(8,128)} %get-tuple-element.15.r_ref), custom_call_target="tpu_custom_call" | custom-call | tf_op jit(solution)/shard_map/solve/pallas_call | solution.py:266

commit v2 on v1

v2 whole, which is shorter than its diff:
```python
import functools

import jax
import jax.numpy as jnp
from jax import lax
from jax.experimental import pallas as pl
from jax.experimental.pallas import tpu as pltpu
from jax.sharding import PartitionSpec as P

F32 = jnp.float32
BF16 = jnp.bfloat16
MESH = pl.DeviceIdType.MESH
NY, NZ = 8, 8
LP = 128
HIGHEST = lax.Precision.HIGHEST


def dot(a, b, dims, precision=None):
    return lax.dot_general(a, b, (dims, ((), ())), precision=precision, preferred_element_type=F32)


def total(terms):
    return functools.reduce(lambda a, b: a + b, terms)


def expand_rows(slow_t, fast_t, width):
    ns, nf = slow_t.shape[0], fast_t.shape[0]
    n = lax.broadcasted_iota(jnp.int32, (ns, width), 1)
    a = lax.broadcasted_iota(jnp.int32, (ns, width), 0)
    pick_slow = jnp.where(n // nf == a, 1.0, 0.0).astype(BF16)
    n = lax.broadcasted_iota(jnp.int32, (nf, width), 1)
    b = lax.broadcasted_iota(jnp.int32, (nf, width), 0)
    pick_fast = jnp.where(n % nf == b, 1.0, 0.0).astype(BF16)
    dims = ((0,), (0,))
    return (dot(slow_t, pick_slow, dims) * dot(fast_t, pick_fast, dims)).astype(BF16)


def sketch_kernel(
    nx, part,
    x_hbm, ls_ref, lf_ref, rs_ref, rf_ref,
    c_out, l_out, r_out,
    xb, psi, omega, acc, ct, rt, lt, cp,
    cc, cs, cy, cq, cz, cr, cx, cf,
    lc, ls, ly, lq, lz,
    ra, rb, rl, rr,
    xsem, ssem, rsem, osem,
):
    cell = lax.axis_index("cells")
    x = lax.axis_index("samp")
    c = lax.rem(cell, 2)
    z = lax.rem(cell // 2, NZ)
    y = cell // (2 * NZ)
    rank_l, rank_r = ls_ref.shape[1], rs_ref.shape[1]
    rows, samples = xb.shape
    pr = cp.shape[2]

    def at(y_, z_, c_, x_):
        return ((y_ * NZ + z_) * 2 + c_, x_)

    other = at(y, z, 1 - c, x)
    ys = [lax.rem(y + d, NY) for d in range(1, NY)]
    zs = [lax.rem(z + d, NZ) for d in range(1, NZ)]
    xs = [lax.rem(x + d, nx) for d in range(1, nx)]
    to_y = [at(p, z, c, x) for p in ys]
    to_z = [at(y, p, c, x) for p in zs]
    to_x = [at(y, z, c, p) for p in xs]
    right, left = to_x[0], to_x[-1]

    loads = []
    for i in range(nx):
        span = pl.ds(i * part, part)
        loads.append(pltpu.make_async_copy(x_hbm.at[span], xb.at[span], xsem.at[i]))
        loads[-1].start()

    barrier = pltpu.get_barrier_semaphore()
    peers = [other] + to_y + to_z + to_x
    for peer in peers:
        pl.semaphore_signal(barrier, inc=1, device_id=peer, device_id_type=MESH)

    used = [0]
    sent = []

    def remote(src, dst, peer):
        k = used[0]
        used[0] += 1
        copy = pltpu.make_async_remote_copy(
            src_ref=src, dst_ref=dst, send_sem=ssem.at[k], recv_sem=rsem.at[k],
            device_id=peer, device_id_type=MESH,
        )
        sent.append(copy)
        return copy

    def send(src, dst, peer):
        copy = remote(src, dst, peer)
        copy.start()
        return copy

    def arrived(copies):
        for copy in copies:
            copy.wait_recv()

    early = z < NZ // 2
    half = part // 2
    lo, hi = pl.ds(0, half), pl.ds(half, half)
    far = lax.rem(x + 2, nx)
    g_ra = remote(rt.at[far, :, lo], ra, right)
    g_rb = remote(rt.at[far, :, hi], rb, left)

    def range_product():
        for i in range(nx):
            rt[i] = dot(omega[...], xb[i * part : (i + 1) * part, :], ((1,), (1,)))

    def range_start():
        g_ra.start()
        g_rb.start()

    psi[...] = expand_rows(ls_ref[...], lf_ref[...], rows)
    omega[...] = expand_rows(rs_ref[...], rf_ref[...], samples)
    for copy in loads:
        copy.wait()

    @pl.when(early)
    def _():
        range_product()

    left_part = dot(psi[...], xb[...], ((1,), (0,)))
    acc[rank_l:, :] = jnp.zeros((LP - rank_l, samples), F32)
    acc[0:rank_l, :] = left_part
    top = left_part.astype(BF16)
    rest = left_part - top.astype(F32)
    mid = rest.astype(BF16)
    low = (rest - mid.astype(F32)).astype(BF16)
    om = omega[...]
    dims = ((1,), (1,))
    ct[...] = jnp.zeros_like(ct)
    ct[0:rank_r, 0:rank_l] = dot(om, top, dims) + (dot(om, mid, dims) + dot(om, low, dims))
    for k in range(2 * NY):
        cp[k // NY, k % NY] = ct[k * pr : (k + 1) * pr, :]

    pl.semaphore_wait(barrier, len(peers))
    g_cc = [send(cp.at[1 - c], cc, other)]

    @pl.when(early)
    def _():
        range_start()

    left_t = acc[...].T
    for j in range(samples // 8):
        lt[j % 2, j // (2 * NZ), (j // 2) % NZ] = left_t[8 * j : 8 * j + 8, :]
    g_lc = [send(lt.at[1 - c], lc, other)]

    arrived(g_cc)
    cs[...] = cp[c] + cc[...]
    g_cy = [send(cs.at[ys[i]], cy.at[i], to_y[i]) for i in range(NY - 1)]

    @pl.when(jnp.logical_not(early))
    def _():
        range_product()
        range_start()

    arrived(g_lc)
    ls[...] = lt[c] + lc[...]
    g_ly = [send(ls.at[ys[i]], ly.at[i], to_y[i]) for i in range(NY - 1)]

    arrived(g_cy)
    cq[...] = cs[y] + total([cy[i] for i in range(NY - 1)])
    g_cz = [send(cq, cz.at[i], to_z[i]) for i in range(NZ - 1)]

    arrived([g_ra, g_rb])
    xr, xl = xs[0], xs[-1]
    rl[:, lo] = rt[xr, :, lo] + ra[...]
    rl[:, hi] = rt[xr, :, hi]
    rr[:, lo] = rt[xl, :, lo]
    rr[:, hi] = rt[xl, :, hi] + rb[...]
    g_r = [send(rl, r_out.at[0], right), send(rr, r_out.at[1], left)]
    own = pltpu.make_async_copy(rt.at[x], r_out.at[2], osem)
    own.start()

    arrived(g_cz)
    cr[...] = cq[...] + total([cz[i] for i in range(NZ - 1)])
    g_cx = [send(cr, cx.at[i], to_x[i]) for i in range(nx - 1)]
    arrived(g_cx)
    cf[c, y] = cr[...] + total([cx[i] for i in range(nx - 1)])
    g_ag = [send(cf.at[c, y], cf.at[c, y], to_y[i]) for i in range(NY - 1)]

    arrived(g_ly)
    lq[...] = ls[y] + total([ly[i] for i in range(NY - 1)])
    g_lz = [send(lq.at[zs[i]], lz.at[i], to_z[i]) for i in range(NZ - 1)]

    arrived(g_ag)
    g_ac = [send(cf.at[c], cf.at[c], other)]

    arrived(g_lz)
    l_out[...] = lq[z] + total([lz[i] for i in range(NZ - 1)])
    arrived(g_ac)
    c_out[...] = cf[...]
    own.wait()
    arrived(g_r)
    for copy in sent:
        copy.wait_send()


def rows_of(a, t):
    return jnp.broadcast_to(a[t : t + 1, :], (8, LP))


def lanes_of(a, t):
    return jnp.broadcast_to(a[:, t : t + 1], (8, LP))


def solve_kernel(rank_l, c_ref, l_ref, r_hbm, core_ref, range_hbm, ct, rbuf, rsum, rsem, wsem):
    fetch = pltpu.make_async_copy(r_hbm, rbuf, rsem)
    fetch.start()
    pr = c_ref.shape[2]
    for k in range(2 * NY):
        ct[k * pr : (k + 1) * pr, :] = c_ref[k // NY, k % NY]
    cm = ct[...]
    gram = dot(cm, cm, ((0,), (0,)), HIGHEST)
    row = lax.broadcasted_iota(jnp.int32, (LP, LP), 0)
    col = lax.broadcasted_iota(jnp.int32, (LP, LP), 1)
    gram = gram + jnp.where(row == col, 0.5, 0.0)
    sub = lax.broadcasted_iota(jnp.int32, (8, LP), 0)
    lane = lax.broadcasted_iota(jnp.int32, (8, LP), 1)

    fetch.wait()
    rsum[...] = rbuf[2] + (rbuf[0] + rbuf[1])
    write = pltpu.make_async_copy(rsum, range_hbm, wsem)
    write.start()

    tiles = [gram[8 * i : 8 * i + 8, :] for i in range(LP // 8)]
    rhs = l_ref[...]
    panels = rank_l // 8
    for kb in range(panels):
        base = 8 * kb
        p = tiles[kb]
        cols = [lanes_of(p, base + t) for t in range(8)]
        for t in range(8):
            ct_ = cols[t]
            inv = 1.0 / rows_of(ct_, t)
            here = lane == base + t
            prow = jnp.where(here, inv, rows_of(p, t) * inv)
            p = jnp.where(sub == t, prow, jnp.where(here, 0.0, p) - ct_ * prow)
            for j in range(t + 1, 8):
                crow = rows_of(cols[j], t) * inv
                cols[j] = jnp.where(sub == t, crow, cols[j] - ct_ * crow)
        inside = (lane >= base) & (lane < base + 8)
        w = jnp.where(inside, -p, p)
        ws = [rows_of(w, t) for t in range(8)]

        def update(a):
            terms = [lanes_of(a, base + t) * ws[t] for t in range(8)]
            while len(terms) > 1:
                terms = [terms[i] + terms[i + 1] for i in range(0, len(terms), 2)]
            return jnp.where(inside, 0.0, a) - terms[0]

        for i in range(kb + 1, panels):
            tiles[i] = update(tiles[i])
        rhs = update(rhs)
    core = dot(rhs, cm, ((1,), (1,)), HIGHEST)
    core_ref[...] = core[:, 0 : core_ref.shape[1]]
    write.wait()


VMEM = pl.BlockSpec(memory_space=pltpu.VMEM)
ANY = pl.BlockSpec(memory_space=pl.ANY)


def on_device(snapshots, left_slow, left_fast, right_slow, right_fast):
    nx = lax.axis_size("samp")
    rows, samples = snapshots.shape
    rank_l, rank_r = left_slow.shape[0], right_slow.shape[0]
    part = rows // nx
    pr = -(-rank_r // (2 * NY))
    f32 = lambda *shape: jax.ShapeDtypeStruct(shape, F32)
    vm = lambda *shape: pltpu.VMEM(shape, F32)
    dma = lambda *shape: pltpu.SemaphoreType.DMA(shape)
    copies = 2 + 4 + 3 * (NY - 1) + 2 * (NZ - 1) + (nx - 1) + 1
    cf, lf, rf = pl.pallas_call(
        functools.partial(sketch_kernel, nx, part),
        in_specs=[ANY] + [VMEM] * 4,
        out_specs=(VMEM, VMEM, ANY),
        out_shape=(f32(2, NY, pr, LP), f32(8, LP), f32(3, rank_r, part)),
        scratch_shapes=[
            pltpu.VMEM((rows, samples), BF16),
            pltpu.VMEM((rank_l, rows), BF16),
            pltpu.VMEM((rank_r, samples), BF16),
            vm(LP, samples), vm(2 * NY * pr, LP), vm(nx, rank_r, part),
            vm(2, NY, NZ, 8, LP), vm(2, NY, pr, LP),
            vm(NY, pr, LP), vm(NY, pr, LP), vm(NY - 1, pr, LP), vm(pr, LP),
            vm(NZ - 1, pr, LP), vm(pr, LP), vm(nx - 1, pr, LP), vm(2, NY, pr, LP),
            vm(NY, NZ, 8, LP), vm(NY, NZ, 8, LP), vm(NY - 1, NZ, 8, LP), vm(NZ, 8, LP),
            vm(NZ - 1, 8, LP),
            vm(rank_r, part // 2), vm(rank_r, part // 2), vm(rank_r, part), vm(rank_r, part),
            dma(nx), dma(copies), dma(copies), pltpu.SemaphoreType.DMA,
        ],
        compiler_params=pltpu.CompilerParams(collective_id=0, has_side_effects=True),
        name="sketch",
    )(snapshots, left_slow.T, left_fast.T, right_slow.T, right_fast.T)

    core_t, range_t = pl.pallas_call(
        functools.partial(solve_kernel, rank_l),
        in_specs=[VMEM, VMEM, ANY],
        out_specs=(VMEM, ANY),
        out_shape=(f32(8, rank_r), f32(rank_r, part)),
        scratch_shapes=[
            vm(2 * NY * pr, LP), vm(3, rank_r, part), vm(rank_r, part),
            pltpu.SemaphoreType.DMA, pltpu.SemaphoreType.DMA,
        ],
        name="solve",
    )(cf, lf, rf)
    return (range_t.T, core_t.T)


def solution(mesh):
    placed = (P("cells", "samp"), P(None, "cells"), P(), P(None, "samp"), P())
    return jax.shard_map(
        on_device,
        mesh=mesh,
        in_specs=placed,
        out_specs=(P(("cells", "samp"), None), P(None, ("samp", "cells"))),
        check_vma=False,
    )
```

time: 54.3 us -> 47.4 us (0.87)
  Pallas kernels: 53.4 us -> 46.5 us
    pallas_call x3 -> x2, Pallas kernels: 53.4 us -> 46.5 us  [the longest x1 38.3 us: on_device(): pl.pallas_call(functools.partial(sketch_kernel, nx, part), in_specs=[ANY]...]
where the time goes in v2:
time: 47.4 us; the launch traced here: 47.1 us
  Pallas kernels  46.5 us (98%)
  between operations  0.64 us (1%)
    pallas_call x1, Pallas kernels, on_device(): pl.pallas_call(functools.partial(sketch_kernel, nx, part), in_specs=[ANY]...  38.3 us
    pallas_call x1, Pallas kernels, on_device(): pl.pallas_call(functools.partial(solve_kernel, rank_l), in_specs=[VMEM, V...  8.14 us

profile of v2, /device:TPU:1, one launch (start us, length us, event | category | flops | bytes accessed | tf_op | source)
XLA Modules:
  0.0 47.1 jit_solution(14600295661503813907)
XLA Ops:
  0.6 38.3 %sketch.1 = (f32[2,8,10,128]{3,2,1,0:T(8,128)}, f32[8,128]{1,0:T(8,128)}, f32[3,150,512]{2,1,0:T(8,128)}) custom-call(bf16[2048,1024]{1,0:T(8,128)(2,1)} %x_hbm.1, bf16[32,120]{1,0:T(8,128)(2,1)} %bitcast.9, bf16[64,120]{1,0:T(8,128)(2,1)} %bitcast.6, bf16[32,150]{1,0:T(8,128)(2,1)} %bitcast.7, bf16[32,150]{1,0:T(8,128)(2,1)} %bitcast.8), custom_call_target="tpu_custom_call" | custom-call | tf_op jit(solution)/shard_map/sketch/pallas_call | solution.py:278
  39.0 8.1 %solve.1 = (f32[8,150]{1,0:T(8,128)}, f32[150,512]{1,0:T(8,128)}) custom-call(f32[2,8,10,128]{3,2,1,0:T(8,128)} %get-tuple-element.7.c_ref, f32[8,128]{1,0:T(8,128)} %get-tuple-element.8.l_ref, f32[3,150,512]{2,1,0:T(8,128)} %get-tuple-element.9.r_hbm), custom_call_target="tpu_custom_call" | custom-call | tf_op jit(solution)/shard_map/solve/pallas_call | solution.py:300

commit v3 on v2

--- a/solution.py
+++ b/solution.py
@@ -37,13 +37,13 @@
 
 def sketch_kernel(
     nx, part,
-    x_hbm, ls_ref, lf_ref, rs_ref, rf_ref,
+    x_hbm, ls_hbm, lf_hbm, rs_hbm, rf_hbm,
     c_out, l_out, r_out,
-    xb, psi, omega, acc, ct, rt, lt, cp,
-    cc, cs, cy, cq, cz, cr, cx, cf,
-    lc, ls, ly, lq, lz,
+    ls_ref, lf_ref, rs_ref, rf_ref, xb, psi, omega, acc, ct, rt, lt, cp,
+    cy, cq, cx, cr, cz, cw,
+    lc, ls, ly, lq, lz, lw,
     ra, rb, rl, rr,
-    xsem, ssem, rsem, osem,
+    xsem, wsem, ssem, rsem, osem,
 ):
     cell = lax.axis_index("cells")
     x = lax.axis_index("samp")
@@ -51,31 +51,39 @@
     z = lax.rem(cell // 2, NZ)
     y = cell // (2 * NZ)
     rank_l, rank_r = ls_ref.shape[1], rs_ref.shape[1]
-    rows, samples = xb.shape
+    samples = xb.shape[1]
     pr = cp.shape[2]
 
     def at(y_, z_, c_, x_):
         return ((y_ * NZ + z_) * 2 + c_, x_)
 
-    other = at(y, z, 1 - c, x)
     ys = [lax.rem(y + d, NY) for d in range(1, NY)]
     zs = [lax.rem(z + d, NZ) for d in range(1, NZ)]
     xs = [lax.rem(x + d, nx) for d in range(1, nx)]
+    other = at(y, z, 1 - c, x)
     to_y = [at(p, z, c, x) for p in ys]
+    to_yc = [at(p, z, 1 - c, x) for p in ys]
     to_z = [at(y, p, c, x) for p in zs]
     to_x = [at(y, z, c, p) for p in xs]
     right, left = to_x[0], to_x[-1]
 
+    barrier = pltpu.get_barrier_semaphore()
+    peers = [other] + to_y + to_yc + to_z + to_x
+    for peer in peers:
+        pl.semaphore_signal(barrier, inc=1, device_id=peer, device_id_type=MESH)
+
+    small = [
+        pltpu.make_async_copy(src, dst, wsem.at[i])
+        for i, (src, dst) in enumerate(
+            [(ls_hbm, ls_ref), (lf_hbm, lf_ref), (rs_hbm, rs_ref), (rf_hbm, rf_ref)]
+        )
+    ]
     loads = []
     for i in range(nx):
         span = pl.ds(i * part, part)
         loads.append(pltpu.make_async_copy(x_hbm.at[span], xb.at[span], xsem.at[i]))
-        loads[-1].start()
-
-    barrier = pltpu.get_barrier_semaphore()
-    peers = [other] + to_y + to_z + to_x
-    for peer in peers:
-        pl.semaphore_signal(barrier, inc=1, device_id=peer, device_id_type=MESH)
+    for copy in small + loads:
+        copy.start()
 
     used = [0]
     sent = []
@@ -100,32 +108,45 @@
             copy.wait_recv()
 
     early = z < NZ // 2
+    late = jnp.logical_not(early)
     half = part // 2
     lo, hi = pl.ds(0, half), pl.ds(half, half)
     far = lax.rem(x + 2, nx)
-    g_ra = remote(rt.at[far, :, lo], ra, right)
-    g_rb = remote(rt.at[far, :, hi], rb, left)
+    xr, xl = xs[0], xs[-1]
+    g_ra = [remote(rt.at[far, :, lo], ra, right), remote(rt.at[far, :, hi], rb, left)]
+    g_r = [remote(rl, r_out.at[0], right), remote(rr, r_out.at[1], left)]
+    own_r = pltpu.make_async_copy(rt.at[x], r_out.at[2], osem.at[0])
 
     def range_product():
         for i in range(nx):
             rt[i] = dot(omega[...], xb[i * part : (i + 1) * part, :], ((1,), (1,)))
 
-    def range_start():
-        g_ra.start()
-        g_rb.start()
-
-    psi[...] = expand_rows(ls_ref[...], lf_ref[...], rows)
+    def range_first():
+        for copy in g_ra:
+            copy.start()
+        own_r.start()
+
+    def range_second():
+        arrived(g_ra)
+        rl[:, lo] = rt[xr, :, lo] + ra[...]
+        rl[:, hi] = rt[xr, :, hi]
+        rr[:, lo] = rt[xl, :, lo]
+        rr[:, hi] = rt[xl, :, hi] + rb[...]
+        for copy in g_r:
+            copy.start()
+
+    for copy in small:
+        copy.wait()
     omega[...] = expand_rows(rs_ref[...], rf_ref[...], samples)
-    for copy in loads:
-        copy.wait()
-
-    @pl.when(early)
-    def _():
-        range_product()
-
-    left_part = dot(psi[...], xb[...], ((1,), (0,)))
+    psi[...] = expand_rows(ls_ref[...], lf_ref[...], nx * part)
     acc[rank_l:, :] = jnp.zeros((LP - rank_l, samples), F32)
-    acc[0:rank_l, :] = left_part
+    for i in range(nx):
+        loads[i].wait()
+        rows = slice(i * part, (i + 1) * part)
+        term = dot(psi[:, rows], xb[rows, :], ((1,), (0,)))
+        acc[0:rank_l, :] = term if i == 0 else acc[0:rank_l, :] + term
+
+    left_part = acc[0:rank_l, :]
     top = left_part.astype(BF16)
     rest = left_part - top.astype(F32)
     mid = rest.astype(BF16)
@@ -137,65 +158,75 @@
     for k in range(2 * NY):
         cp[k // NY, k % NY] = ct[k * pr : (k + 1) * pr, :]
 
+    @pl.when(early)
+    def _():
+        range_product()
+
     pl.semaphore_wait(barrier, len(peers))
-    g_cc = [send(cp.at[1 - c], cc, other)]
+
+    g_cy = [send(cp.at[c, ys[i]], cy.at[i], to_y[i]) for i in range(NY - 1)]
+    g_cy += [send(cp.at[1 - c, ys[i]], cy.at[NY - 1 + i], to_yc[i]) for i in range(NY - 1)]
+    g_cy += [send(cp.at[1 - c, y], cy.at[2 * NY - 2], other)]
 
     @pl.when(early)
     def _():
-        range_start()
+        range_first()
 
     left_t = acc[...].T
     for j in range(samples // 8):
         lt[j % 2, j // (2 * NZ), (j // 2) % NZ] = left_t[8 * j : 8 * j + 8, :]
     g_lc = [send(lt.at[1 - c], lc, other)]
 
-    arrived(g_cc)
-    cs[...] = cp[c] + cc[...]
-    g_cy = [send(cs.at[ys[i]], cy.at[i], to_y[i]) for i in range(NY - 1)]
-
-    @pl.when(jnp.logical_not(early))
+    @pl.when(late)
     def _():
         range_product()
-        range_start()
 
     arrived(g_lc)
     ls[...] = lt[c] + lc[...]
+
+    @pl.when(early)
+    def _():
+        range_second()
+
+    arrived(g_cy)
+    cq[...] = cp[c, y] + total([cy[i] for i in range(2 * NY - 1)])
+    g_cx = [send(cq, cx.at[i], to_x[i]) for i in range(nx - 1)]
+
+    @pl.when(late)
+    def _():
+        range_first()
+
     g_ly = [send(ls.at[ys[i]], ly.at[i], to_y[i]) for i in range(NY - 1)]
 
-    arrived(g_cy)
-    cq[...] = cs[y] + total([cy[i] for i in range(NY - 1)])
-    g_cz = [send(cq, cz.at[i], to_z[i]) for i in range(NZ - 1)]
-
-    arrived([g_ra, g_rb])
-    xr, xl = xs[0], xs[-1]
-    rl[:, lo] = rt[xr, :, lo] + ra[...]
-    rl[:, hi] = rt[xr, :, hi]
-    rr[:, lo] = rt[xl, :, lo]
-    rr[:, hi] = rt[xl, :, hi] + rb[...]
-    g_r = [send(rl, r_out.at[0], right), send(rr, r_out.at[1], left)]
-    own = pltpu.make_async_copy(rt.at[x], r_out.at[2], osem)
-    own.start()
+    arrived(g_cx)
+    cr[...] = cq[...] + total([cx[i] for i in range(nx - 1)])
+    g_cz = [send(cr, cz.at[i], to_z[i]) for i in range(NZ - 1)]
+
+    @pl.when(late)
+    def _():
+        range_second()
 
     arrived(g_cz)
-    cr[...] = cq[...] + total([cz[i] for i in range(NZ - 1)])
-    g_cx = [send(cr, cx.at[i], to_x[i]) for i in range(nx - 1)]
-    arrived(g_cx)
-    cf[c, y] = cr[...] + total([cx[i] for i in range(nx - 1)])
-    g_ag = [send(cf.at[c, y], cf.at[c, y], to_y[i]) for i in range(NY - 1)]
+    cw[...] = cr[...] + total([cz[i] for i in range(NZ - 1)])
+    g_ag = [send(cw, c_out.at[c, y], to_y[i]) for i in range(NY - 1)]
+    g_ag += [send(cw, c_out.at[c, y], to_yc[i]) for i in range(NY - 1)]
+    g_ag += [send(cw, c_out.at[c, y], other)]
+    own_c = pltpu.make_async_copy(cw, c_out.at[c, y], osem.at[1])
+    own_c.start()
 
     arrived(g_ly)
     lq[...] = ls[y] + total([ly[i] for i in range(NY - 1)])
     g_lz = [send(lq.at[zs[i]], lz.at[i], to_z[i]) for i in range(NZ - 1)]
-
+    arrived(g_lz)
+    lw[...] = lq[z] + total([lz[i] for i in range(NZ - 1)])
+    own_l = pltpu.make_async_copy(lw, l_out, osem.at[2])
+    own_l.start()
+
+    own_r.wait()
+    own_c.wait()
+    arrived(g_r)
     arrived(g_ag)
-    g_ac = [send(cf.at[c], cf.at[c], other)]
-
-    arrived(g_lz)
-    l_out[...] = lq[z] + total([lz[i] for i in range(NZ - 1)])
-    arrived(g_ac)
-    c_out[...] = cf[...]
-    own.wait()
-    arrived(g_r)
+    own_l.wait()
     for copy in sent:
         copy.wait_send()
 
@@ -274,28 +305,29 @@
     f32 = lambda *shape: jax.ShapeDtypeStruct(shape, F32)
     vm = lambda *shape: pltpu.VMEM(shape, F32)
     dma = lambda *shape: pltpu.SemaphoreType.DMA(shape)
-    copies = 2 + 4 + 3 * (NY - 1) + 2 * (NZ - 1) + (nx - 1) + 1
+    copies = 4 + 2 * (2 * NY - 1) + (nx - 1) + (NZ - 1) + 1 + (NY - 1) + (NZ - 1)
+    small = [left_slow.T, left_fast.T, right_slow.T, right_fast.T]
     cf, lf, rf = pl.pallas_call(
         functools.partial(sketch_kernel, nx, part),
-        in_specs=[ANY] + [VMEM] * 4,
-        out_specs=(VMEM, VMEM, ANY),
+        in_specs=[ANY] * 5,
+        out_specs=(ANY,) * 3,
         out_shape=(f32(2, NY, pr, LP), f32(8, LP), f32(3, rank_r, part)),
-        scratch_shapes=[
+        scratch_shapes=[pltpu.VMEM(a.shape, BF16) for a in small] + [
             pltpu.VMEM((rows, samples), BF16),
             pltpu.VMEM((rank_l, rows), BF16),
             pltpu.VMEM((rank_r, samples), BF16),
             vm(LP, samples), vm(2 * NY * pr, LP), vm(nx, rank_r, part),
             vm(2, NY, NZ, 8, LP), vm(2, NY, pr, LP),
-            vm(NY, pr, LP), vm(NY, pr, LP), vm(NY - 1, pr, LP), vm(pr, LP),
-            vm(NZ - 1, pr, LP), vm(pr, LP), vm(nx - 1, pr, LP), vm(2, NY, pr, LP),
+            vm(2 * NY - 1, pr, LP), vm(pr, LP), vm(nx - 1, pr, LP), vm(pr, LP),
+            vm(NZ - 1, pr, LP), vm(pr, LP),
             vm(NY, NZ, 8, LP), vm(NY, NZ, 8, LP), vm(NY - 1, NZ, 8, LP), vm(NZ, 8, LP),
-            vm(NZ - 1, 8, LP),
+            vm(NZ - 1, 8, LP), vm(8, LP),
             vm(rank_r, part // 2), vm(rank_r, part // 2), vm(rank_r, part), vm(rank_r, part),
-            dma(nx), dma(copies), dma(copies), pltpu.SemaphoreType.DMA,
+            dma(nx), dma(4), dma(copies), dma(copies), dma(3),
         ],
         compiler_params=pltpu.CompilerParams(collective_id=0, has_side_effects=True),
         name="sketch",
-    )(snapshots, left_slow.T, left_fast.T, right_slow.T, right_fast.T)
+    )(snapshots, *small)
 
     core_t, range_t = pl.pallas_call(
         functools.partial(solve_kernel, rank_l),

time: 47.4 us -> 49.1 us (1.036)
  Pallas kernels: 46.5 us -> 48.2 us
    pallas_call x1, Pallas kernels: 38.3 us -> 40 us  [on_device(): pl.pallas_call(functools.partial(sketch_kernel, nx, part), in_specs=[ANY]...]
where the time goes in v3:
time: 49.1 us; the launch traced here: 48.8 us
  Pallas kernels  48.2 us (98%)
  between operations  0.64 us (1%)
    pallas_call x1, Pallas kernels, on_device(): pl.pallas_call(functools.partial(sketch_kernel, nx, part), in_specs=[ANY]...  40 us
    pallas_call x1, Pallas kernels, on_device(): pl.pallas_call(functools.partial(solve_kernel, rank_l), in_specs=[VMEM, V...  8.14 us

profile of v3, /device:TPU:1, one launch (start us, length us, event | category | flops | bytes accessed | tf_op | source)
XLA Modules:
  0.0 48.8 jit_solution(8279762195566960909)
XLA Ops:
  0.6 40.0 %sketch.1 = (f32[2,8,10,128]{3,2,1,0:T(8,128)}, f32[8,128]{1,0:T(8,128)}, f32[3,150,512]{2,1,0:T(8,128)}) custom-call(bf16[2048,1024]{1,0:T(8,128)(2,1)} %x_hbm.1, bf16[32,120]{1,0:T(8,128)(2,1)} %bitcast.9, bf16[64,120]{1,0:T(8,128)(2,1)} %bitcast.6, bf16[32,150]{1,0:T(8,128)(2,1)} %bitcast.7, bf16[32,150]{1,0:T(8,128)(2,1)} %bitcast.8), custom_call_target="tpu_custom_call" | custom-call | tf_op jit(solution)/shard_map/sketch/pallas_call | solution.py:310
  40.7 8.1 %solve.1 = (f32[8,150]{1,0:T(8,128)}, f32[150,512]{1,0:T(8,128)}) custom-call(f32[2,8,10,128]{3,2,1,0:T(8,128)} %get-tuple-element.7.c_ref, f32[8,128]{1,0:T(8,128)} %get-tuple-element.8.l_ref, f32[3,150,512]{2,1,0:T(8,128)} %get-tuple-element.9.r_hbm), custom_call_target="tpu_custom_call" | custom-call | tf_op jit(solution)/shard_map/solve/pallas_call | solution.py:332

commit v4 on v3

--- a/solution.py
+++ b/solution.py
@@ -42,7 +42,7 @@
     ls_ref, lf_ref, rs_ref, rf_ref, xb, psi, omega, acc, ct, rt, lt, cp,
     cy, cq, cx, cr, cz, cw,
     lc, ls, ly, lq, lz, lw,
-    ra, rb, rl, rr,
+    ra, rb, rl, rr, rf, rsum,
     xsem, wsem, ssem, rsem, osem,
 ):
     cell = lax.axis_index("cells")
@@ -114,8 +114,8 @@
     far = lax.rem(x + 2, nx)
     xr, xl = xs[0], xs[-1]
     g_ra = [remote(rt.at[far, :, lo], ra, right), remote(rt.at[far, :, hi], rb, left)]
-    g_r = [remote(rl, r_out.at[0], right), remote(rr, r_out.at[1], left)]
-    own_r = pltpu.make_async_copy(rt.at[x], r_out.at[2], osem.at[0])
+    g_r = [remote(rl, rf.at[0], right), remote(rr, rf.at[1], left)]
+    own_r = pltpu.make_async_copy(rsum, r_out, osem.at[0])
 
     def range_product():
         for i in range(nx):
@@ -124,7 +124,6 @@
     def range_first():
         for copy in g_ra:
             copy.start()
-        own_r.start()
 
     def range_second():
         arrived(g_ra)
@@ -184,13 +183,13 @@
     arrived(g_lc)
     ls[...] = lt[c] + lc[...]
 
-    @pl.when(early)
-    def _():
-        range_second()
-
     arrived(g_cy)
     cq[...] = cp[c, y] + total([cy[i] for i in range(2 * NY - 1)])
     g_cx = [send(cq, cx.at[i], to_x[i]) for i in range(nx - 1)]
+
+    @pl.when(early)
+    def _():
+        range_second()
 
     @pl.when(late)
     def _():
@@ -217,6 +216,9 @@
     arrived(g_ly)
     lq[...] = ls[y] + total([ly[i] for i in range(NY - 1)])
     g_lz = [send(lq.at[zs[i]], lz.at[i], to_z[i]) for i in range(NZ - 1)]
+    arrived(g_r)
+    rsum[...] = rt[x] + (rf[0] + rf[1])
+    own_r.start()
     arrived(g_lz)
     lw[...] = lq[z] + total([lz[i] for i in range(NZ - 1)])
     own_l = pltpu.make_async_copy(lw, l_out, osem.at[2])
@@ -224,7 +226,6 @@
 
     own_r.wait()
     own_c.wait()
-    arrived(g_r)
     arrived(g_ag)
     own_l.wait()
     for copy in sent:
@@ -239,7 +240,7 @@
     return jnp.broadcast_to(a[:, t : t + 1], (8, LP))
 
 
-def solve_kernel(rank_l, c_ref, l_ref, r_hbm, core_ref, range_hbm, ct, rbuf, rsum, rsem, wsem):
+def solve_kernel(rank_l, c_ref, l_ref, r_hbm, core_ref, range_hbm, ct, rbuf, rsem, wsem):
     fetch = pltpu.make_async_copy(r_hbm, rbuf, rsem)
     fetch.start()
     pr = c_ref.shape[2]
@@ -253,11 +254,7 @@
     sub = lax.broadcasted_iota(jnp.int32, (8, LP), 0)
     lane = lax.broadcasted_iota(jnp.int32, (8, LP), 1)
 
-    fetch.wait()
-    rsum[...] = rbuf[2] + (rbuf[0] + rbuf[1])
-    write = pltpu.make_async_copy(rsum, range_hbm, wsem)
-    write.start()
-
+    write = pltpu.make_async_copy(rbuf, range_hbm, wsem)
     tiles = [gram[8 * i : 8 * i + 8, :] for i in range(LP // 8)]
     rhs = l_ref[...]
     panels = rank_l // 8
@@ -287,6 +284,9 @@
         for i in range(kb + 1, panels):
             tiles[i] = update(tiles[i])
         rhs = update(rhs)
+        if kb == panels // 2:
+            fetch.wait()
+            write.start()
     core = dot(rhs, cm, ((1,), (1,)), HIGHEST)
     core_ref[...] = core[:, 0 : core_ref.shape[1]]
     write.wait()
@@ -311,7 +311,7 @@
         functools.partial(sketch_kernel, nx, part),
         in_specs=[ANY] * 5,
         out_specs=(ANY,) * 3,
-        out_shape=(f32(2, NY, pr, LP), f32(8, LP), f32(3, rank_r, part)),
+        out_shape=(f32(2, NY, pr, LP), f32(8, LP), f32(rank_r, part)),
         scratch_shapes=[pltpu.VMEM(a.shape, BF16) for a in small] + [
             pltpu.VMEM((rows, samples), BF16),
             pltpu.VMEM((rank_l, rows), BF16),
@@ -323,6 +323,7 @@
             vm(NY, NZ, 8, LP), vm(NY, NZ, 8, LP), vm(NY - 1, NZ, 8, LP), vm(NZ, 8, LP),
             vm(NZ - 1, 8, LP), vm(8, LP),
             vm(rank_r, part // 2), vm(rank_r, part // 2), vm(rank_r, part), vm(rank_r, part),
+            vm(2, rank_r, part), vm(rank_r, part),
             dma(nx), dma(4), dma(copies), dma(copies), dma(3),
         ],
         compiler_params=pltpu.CompilerParams(collective_id=0, has_side_effects=True),
@@ -335,7 +336,7 @@
         out_specs=(VMEM, ANY),
         out_shape=(f32(8, rank_r), f32(rank_r, part)),
         scratch_shapes=[
-            vm(2 * NY * pr, LP), vm(3, rank_r, part), vm(rank_r, part),
+            vm(2 * NY * pr, LP), vm(rank_r, part),
             pltpu.SemaphoreType.DMA, pltpu.SemaphoreType.DMA,
         ],
         name="solve",

time: 49.1 us -> 41.9 us (0.85)
  Pallas kernels: 48.2 us -> 41 us
    pallas_call x1, Pallas kernels: 40 us -> 34.7 us  [on_device(): pl.pallas_call(functools.partial(sketch_kernel, nx, part), in_specs=[ANY]...]
    pallas_call x1, Pallas kernels: 8.14 us -> 6.33 us  [on_device(): pl.pallas_call(functools.partial(solve_kernel, rank_l), in_specs=[VMEM, V...]
where the time goes in v4:
time: 41.9 us; the launch traced here: 41.7 us
  Pallas kernels  41 us (98%)
  between operations  0.64 us (2%)
    pallas_call x1, Pallas kernels, on_device(): pl.pallas_call(functools.partial(sketch_kernel, nx, part), in_specs=[ANY]...  34.7 us
    pallas_call x1, Pallas kernels, on_device(): pl.pallas_call(functools.partial(solve_kernel, rank_l), in_specs=[VMEM, V...  6.33 us

profile of v4, /device:TPU:1, one launch (start us, length us, event | category | flops | bytes accessed | tf_op | source)
XLA Modules:
  0.0 41.7 jit_solution(11963431657922792103)
XLA Ops:
  0.6 34.7 %sketch.1 = (f32[2,8,10,128]{3,2,1,0:T(8,128)}, f32[8,128]{1,0:T(8,128)}, f32[150,512]{1,0:T(8,128)}) custom-call(bf16[2048,1024]{1,0:T(8,128)(2,1)} %x_hbm.1, bf16[32,120]{1,0:T(8,128)(2,1)} %bitcast.9, bf16[64,120]{1,0:T(8,128)(2,1)} %bitcast.6, bf16[32,150]{1,0:T(8,128)(2,1)} %bitcast.7, bf16[32,150]{1,0:T(8,128)(2,1)} %bitcast.8), custom_call_target="tpu_custom_call" | custom-call | tf_op jit(solution)/shard_map/sketch/pallas_call | solution.py:310
  35.3 6.3 %solve.1 = (f32[8,150]{1,0:T(8,128)}, f32[150,512]{1,0:T(8,128)}) custom-call(f32[2,8,10,128]{3,2,1,0:T(8,128)} %get-tuple-element.7.c_ref, f32[8,128]{1,0:T(8,128)} %get-tuple-element.8.l_ref, f32[150,512]{1,0:T(8,128)} %get-tuple-element.9.r_hbm), custom_call_target="tpu_custom_call" | custom-call | tf_op jit(solution)/shard_map/solve/pallas_call | solution.py:333

commit v5 on v4

--- a/solution.py
+++ b/solution.py
@@ -326,9 +326,11 @@
             vm(2, rank_r, part), vm(rank_r, part),
             dma(nx), dma(4), dma(copies), dma(copies), dma(3),
         ],
-        compiler_params=pltpu.CompilerParams(collective_id=0, has_side_effects=True),
+        compiler_params=pltpu.CompilerParams(
+            collective_id=0, has_side_effects=True, vmem_limit_bytes=24 << 20
+        ),
         name="sketch",
-    )(snapshots, *small)
+    )(*[pltpu.with_memory_space_constraint(a, pltpu.HBM) for a in [snapshots] + small])
 
     core_t, range_t = pl.pallas_call(
         functools.partial(solve_kernel, rank_l),
@@ -339,6 +341,7 @@
             vm(2 * NY * pr, LP), vm(rank_r, part),
             pltpu.SemaphoreType.DMA, pltpu.SemaphoreType.DMA,
         ],
+        compiler_params=pltpu.CompilerParams(vmem_limit_bytes=8 << 20),
         name="solve",
     )(cf, lf, rf)
     return (range_t.T, core_t.T)

time: 41.9 us -> 39.9 us (0.952)
  Pallas kernels: 41 us -> 39.2 us
    pallas_call x1, Pallas kernels: 6.33 us -> 4.94 us  [on_device(): pl.pallas_call(functools.partial(solve_kernel, rank_l), in_specs=[VMEM, V...]
    pallas_call x1, Pallas kernels: 34.7 us -> 34.2 us  [on_device(): pl.pallas_call(functools.partial(sketch_kernel, nx, part), in_specs=[ANY]...]
where the time goes in v5:
time: 39.9 us; the launch traced here: 39.8 us
  Pallas kernels  39.2 us (98%)
  between operations  0.64 us (2%)
    pallas_call x1, Pallas kernels, on_device(): pl.pallas_call(functools.partial(sketch_kernel, nx, part), in_specs=[ANY]...  34.2 us
    pallas_call x1, Pallas kernels, on_device(): pl.pallas_call(functools.partial(solve_kernel, rank_l), in_specs=[VMEM, V...  4.94 us

profile of v5, /device:TPU:1, one launch (start us, length us, event | category | flops | bytes accessed | tf_op | source)
XLA Modules:
  0.0 39.8 jit_solution(14946868637889852874)
XLA Ops:
  0.6 34.2 %sketch.1 = (f32[2,8,10,128]{3,2,1,0:T(8,128)S(1)}, f32[8,128]{1,0:T(8,128)S(1)}, f32[150,512]{1,0:T(8,128)S(1)}) custom-call(bf16[2048,1024]{1,0:T(8,128)(2,1)} %x_hbm.1, bf16[32,120]{1,0:T(8,128)(2,1)} %bitcast.9, bf16[64,120]{1,0:T(8,128)(2,1)} %bitcast.6, bf16[32,150]{1,0:T(8,128)(2,1)} %bitcast.7, bf16[32,150]{1,0:T(8,128)(2,1)} %bitcast.8), custom_call_target="tpu_custom_call" | custom-call | tf_op jit(solution)/shard_map/sketch/pallas_call | solution.py:310
  34.9 4.9 %solve.1 = (f32[8,150]{1,0:T(8,128)}, f32[150,512]{1,0:T(8,128)}) custom-call(f32[2,8,10,128]{3,2,1,0:T(8,128)S(1)} %get-tuple-element.7.c_ref, f32[8,128]{1,0:T(8,128)S(1)} %get-tuple-element.8.l_ref, f32[150,512]{1,0:T(8,128)S(1)} %get-tuple-element.9.r_hbm), custom_call_target="tpu_custom_call" | custom-call | tf_op jit(solution)/shard_map/solve/pallas_call | solution.py:335

commit v6 on v5

--- a/solution.py
+++ b/solution.py
@@ -17,6 +17,10 @@
 
 def dot(a, b, dims, precision=None):
     return lax.dot_general(a, b, (dims, ((), ())), precision=precision, preferred_element_type=F32)
+
+
+def far_first(n):
+    return sorted(range(n - 1), key=lambda i: -min(i + 1, n - 1 - i))
 
 
 def total(terms):
@@ -163,9 +167,11 @@
 
     pl.semaphore_wait(barrier, len(peers))
 
-    g_cy = [send(cp.at[c, ys[i]], cy.at[i], to_y[i]) for i in range(NY - 1)]
-    g_cy += [send(cp.at[1 - c, ys[i]], cy.at[NY - 1 + i], to_yc[i]) for i in range(NY - 1)]
-    g_cy += [send(cp.at[1 - c, y], cy.at[2 * NY - 2], other)]
+    g_cy = []
+    for i in far_first(NY):
+        g_cy.append(send(cp.at[c, ys[i]], cy.at[i], to_y[i]))
+        g_cy.append(send(cp.at[1 - c, ys[i]], cy.at[NY - 1 + i], to_yc[i]))
+    g_cy.append(send(cp.at[1 - c, y], cy.at[2 * NY - 2], other))
 
     @pl.when(early)
     def _():
@@ -185,7 +191,7 @@
 
     arrived(g_cy)
     cq[...] = cp[c, y] + total([cy[i] for i in range(2 * NY - 1)])
-    g_cx = [send(cq, cx.at[i], to_x[i]) for i in range(nx - 1)]
+    g_cx = [send(cq, cx.at[i], to_x[i]) for i in far_first(nx)]
 
     @pl.when(early)
     def _():
@@ -199,7 +205,7 @@
 
     arrived(g_cx)
     cr[...] = cq[...] + total([cx[i] for i in range(nx - 1)])
-    g_cz = [send(cr, cz.at[i], to_z[i]) for i in range(NZ - 1)]
+    g_cz = [send(cr, cz.at[i], to_z[i]) for i in far_first(NZ)]
 
     @pl.when(late)
     def _():
@@ -207,9 +213,10 @@
 
     arrived(g_cz)
     cw[...] = cr[...] + total([cz[i] for i in range(NZ - 1)])
-    g_ag = [send(cw, c_out.at[c, y], to_y[i]) for i in range(NY - 1)]
-    g_ag += [send(cw, c_out.at[c, y], to_yc[i]) for i in range(NY - 1)]
-    g_ag += [send(cw, c_out.at[c, y], other)]
+    g_ag = []
+    for i in far_first(NY):
+        g_ag += [send(cw, c_out.at[c, y], peer) for peer in (to_y[i], to_yc[i])]
+    g_ag.append(send(cw, c_out.at[c, y], other))
     own_c = pltpu.make_async_copy(cw, c_out.at[c, y], osem.at[1])
     own_c.start()
 
@@ -240,9 +247,9 @@
     return jnp.broadcast_to(a[:, t : t + 1], (8, LP))
 
 
-def solve_kernel(rank_l, c_ref, l_ref, r_hbm, core_ref, range_hbm, ct, rbuf, rsem, wsem):
-    fetch = pltpu.make_async_copy(r_hbm, rbuf, rsem)
-    fetch.start()
+def solve_kernel(rank_l, c_ref, l_ref, r_hbm, core_ref, range_hbm, ct, wsem, fence):
+    write = pltpu.make_async_copy(r_hbm, range_hbm, wsem)
+    write.start()
     pr = c_ref.shape[2]
     for k in range(2 * NY):
         ct[k * pr : (k + 1) * pr, :] = c_ref[k // NY, k % NY]
@@ -254,9 +261,7 @@
     sub = lax.broadcasted_iota(jnp.int32, (8, LP), 0)
     lane = lax.broadcasted_iota(jnp.int32, (8, LP), 1)
 
-    write = pltpu.make_async_copy(rbuf, range_hbm, wsem)
-    tiles = [gram[8 * i : 8 * i + 8, :] for i in range(LP // 8)]
-    rhs = l_ref[...]
+    tiles = [gram[8 * i : 8 * i + 8, :] for i in range(rank_l // 8)] + [l_ref[...]]
     panels = rank_l // 8
     for kb in range(panels):
         base = 8 * kb
@@ -275,18 +280,16 @@
         w = jnp.where(inside, -p, p)
         ws = [rows_of(w, t) for t in range(8)]
 
-        def update(a):
-            terms = [lanes_of(a, base + t) * ws[t] for t in range(8)]
-            while len(terms) > 1:
-                terms = [terms[i] + terms[i + 1] for i in range(0, len(terms), 2)]
-            return jnp.where(inside, 0.0, a) - terms[0]
-
-        for i in range(kb + 1, panels):
-            tiles[i] = update(tiles[i])
-        rhs = update(rhs)
-        if kb == panels // 2:
-            fetch.wait()
-            write.start()
+        olds = tiles[kb + 1 :]
+        news = [jnp.where(inside, 0.0, a) for a in olds]
+        for group in ([0], range(1, len(olds))):
+            for t in range(8):
+                for i in group:
+                    news[i] = news[i] - lanes_of(olds[i], base + t) * ws[t]
+        tiles[kb + 1 :] = news
+        pl.semaphore_signal(fence, 1)
+        pl.semaphore_wait(fence, 1)
+    rhs = tiles[panels]
     core = dot(rhs, cm, ((1,), (1,)), HIGHEST)
     core_ref[...] = core[:, 0 : core_ref.shape[1]]
     write.wait()
@@ -338,8 +341,7 @@
         out_specs=(VMEM, ANY),
         out_shape=(f32(8, rank_r), f32(rank_r, part)),
         scratch_shapes=[
-            vm(2 * NY * pr, LP), vm(rank_r, part),
-            pltpu.SemaphoreType.DMA, pltpu.SemaphoreType.DMA,
+            vm(2 * NY * pr, LP), pltpu.SemaphoreType.DMA, pltpu.SemaphoreType.REGULAR,
         ],
         compiler_params=pltpu.CompilerParams(vmem_limit_bytes=8 << 20),
         name="solve",

time: 39.9 us -> 39.2 us (0.982)
  Pallas kernels: 39.2 us -> 38.4 us
where the time goes in v6:
time: 39.2 us; the launch traced here: 39.1 us
  Pallas kernels  38.4 us (98%)
  between operations  0.64 us (2%)
    pallas_call x1, Pallas kernels, on_device(): pl.pallas_call(functools.partial(sketch_kernel, nx, part), in_specs=[ANY]...  33.9 us
    pallas_call x1, Pallas kernels, on_device(): pl.pallas_call(functools.partial(solve_kernel, rank_l), in_specs=[VMEM, V...  4.57 us

profile of v6, /device:TPU:1, one launch (start us, length us, event | category | flops | bytes accessed | tf_op | source)
XLA Modules:
  0.0 39.1 jit_solution(448420021232482176)
XLA Ops:
  0.6 33.9 %sketch.1 = (f32[2,8,10,128]{3,2,1,0:T(8,128)S(1)}, f32[8,128]{1,0:T(8,128)S(1)}, f32[150,512]{1,0:T(8,128)S(1)}) custom-call(bf16[2048,1024]{1,0:T(8,128)(2,1)} %x_hbm.1, bf16[32,120]{1,0:T(8,128)(2,1)} %bitcast.9, bf16[64,120]{1,0:T(8,128)(2,1)} %bitcast.6, bf16[32,150]{1,0:T(8,128)(2,1)} %bitcast.7, bf16[32,150]{1,0:T(8,128)(2,1)} %bitcast.8), custom_call_target="tpu_custom_call" | custom-call | tf_op jit(solution)/shard_map/sketch/pallas_call | solution.py:313
  34.5 4.6 %solve.1 = (f32[8,150]{1,0:T(8,128)}, f32[150,512]{1,0:T(8,128)}) custom-call(f32[2,8,10,128]{3,2,1,0:T(8,128)S(1)} %get-tuple-element.7.c_ref, f32[8,128]{1,0:T(8,128)S(1)} %get-tuple-element.8.l_ref, f32[150,512]{1,0:T(8,128)S(1)} %get-tuple-element.9.r_hbm), custom_call_target="tpu_custom_call" | custom-call | tf_op jit(solution)/shard_map/solve/pallas_call | solution.py:338

commit v7 on v6

--- a/solution.py
+++ b/solution.py
@@ -149,15 +149,14 @@
         term = dot(psi[:, rows], xb[rows, :], ((1,), (0,)))
         acc[0:rank_l, :] = term if i == 0 else acc[0:rank_l, :] + term
 
-    left_part = acc[0:rank_l, :]
+    left_part = acc[...]
     top = left_part.astype(BF16)
     rest = left_part - top.astype(F32)
     mid = rest.astype(BF16)
     low = (rest - mid.astype(F32)).astype(BF16)
-    om = omega[...]
-    dims = ((1,), (1,))
-    ct[...] = jnp.zeros_like(ct)
-    ct[0:rank_r, 0:rank_l] = dot(om, top, dims) + (dot(om, mid, dims) + dot(om, low, dims))
+    terms = dot(omega[...], jnp.concatenate([top, mid, low], axis=0), ((1,), (1,)))
+    ct[rank_r:, :] = jnp.zeros((ct.shape[0] - rank_r, LP), F32)
+    ct[0:rank_r, :] = terms[:, 0:LP] + (terms[:, LP : 2 * LP] + terms[:, 2 * LP :])
     for k in range(2 * NY):
         cp[k // NY, k % NY] = ct[k * pr : (k + 1) * pr, :]
 

time: 39.2 us -> 39.3 us (level)
  no operation moved by 1% of the time
where the time goes in v7:
time: 39.3 us; the launch traced here: 39.2 us
  Pallas kernels  38.5 us (98%)
  between operations  0.64 us (2%)
    pallas_call x1, Pallas kernels, on_device(): pl.pallas_call(functools.partial(sketch_kernel, nx, part), in_specs=[ANY]...  34 us
    pallas_call x1, Pallas kernels, on_device(): pl.pallas_call(functools.partial(solve_kernel, rank_l), in_specs=[VMEM, V...  4.57 us

profile of v7, /device:TPU:1, one launch (start us, length us, event | category | flops | bytes accessed | tf_op | source)
XLA Modules:
  0.0 39.2 jit_solution(15744661245092816736)
XLA Ops:
  0.6 34.0 %sketch.1 = (f32[2,8,10,128]{3,2,1,0:T(8,128)S(1)}, f32[8,128]{1,0:T(8,128)S(1)}, f32[150,512]{1,0:T(8,128)S(1)}) custom-call(bf16[2048,1024]{1,0:T(8,128)(2,1)} %x_hbm.1, bf16[32,120]{1,0:T(8,128)(2,1)} %bitcast.9, bf16[64,120]{1,0:T(8,128)(2,1)} %bitcast.6, bf16[32,150]{1,0:T(8,128)(2,1)} %bitcast.7, bf16[32,150]{1,0:T(8,128)(2,1)} %bitcast.8), custom_call_target="tpu_custom_call" | custom-call | tf_op jit(solution)/shard_map/sketch/pallas_call | solution.py:312
  34.6 4.6 %solve.1 = (f32[8,150]{1,0:T(8,128)}, f32[150,512]{1,0:T(8,128)}) custom-call(f32[2,8,10,128]{3,2,1,0:T(8,128)S(1)} %get-tuple-element.7.c_ref, f32[8,128]{1,0:T(8,128)S(1)} %get-tuple-element.8.l_ref, f32[150,512]{1,0:T(8,128)S(1)} %get-tuple-element.9.r_hbm), custom_call_target="tpu_custom_call" | custom-call | tf_op jit(solution)/shard_map/solve/pallas_call | solution.py:337
